TPU v7x, 256 devices: a whole 4x4x8 slice. The times are simulated.
256 devices in a mesh: band: 64 (over z, y, core), field: 4 (over x).
Axes of the slice: x: 4, y: 4, z: 8, core: 2. Of those that a mesh axis runs over, the one named last changes fastest.
Arguments:
- right_side: float32 [640, 2, 4, 12, 640], P('band', None, 'field'), may hold values from -40 to 40
- legendre: bfloat16 [640, 640, 640], P('band'), may hold values from -0.25 to 0.25
- wave_map: int32 [640], replicated, may hold values from 0 to 639, as said below
- obs_weight: float32 [640, 1280], P('band'), may hold values from 0.2 to 5
Outputs:
- solution: float32 [640, 2, 4, 12, 640], P('band', None, 'field')
- residual: float32 [640, 2, 4, 12, 640], P('band', None, 'field')
Inputs may be any that keep to these rules, and one draw needn't show every extreme that they name: A permutation of 0 to 639; wave_map[s] lies in the same aligned block of 20 values as 639-s.
All inputs are finite; a program needn't handle non-finite values.
Results may differ from a plain program's by a relative error of at most 0.03.
Values may be sent and summed in bfloat16 or wider, within the bound.
A program may use at most 128 MiB of HBM per device.

v0:
```python
import functools
import math

import jax
import jax.numpy as jnp
from jax import lax
from jax.sharding import Mesh
from jax.sharding import PartitionSpec as P

ITERS = 3
BAND_FIELD = ("band_0", "band_1", "band_2", "field")
BAND = ("band_0", "band_1", "band_2")


def by_axis(array, axes):
    return functools.reduce(lax.psum, axes, array)


def triangle_of(own_waves, degrees):
    return (jnp.arange(degrees, dtype=jnp.int32)[None, :] >= own_waves[:, None]).astype(jnp.float32)


def fourier_of(wave_map, lon_count):
    longitude = jnp.arange(lon_count, dtype=jnp.int32)
    phase_int = wave_map[:, None] * longitude[None, :] % lon_count
    angles = phase_int.astype(jnp.float32) * (2.0 * math.pi / lon_count)
    norm_factor = 1.0 / math.sqrt(wave_map.shape[0])
    return (jnp.stack([jnp.cos(angles), -jnp.sin(angles)], axis=1) * norm_factor).astype(
        jnp.bfloat16
    )


def grid_round(spread, fourier_flat, obs_weight):
    slots, parts, items, single, lat_rows = spread.shape
    flat = spread.reshape(slots * parts, items * single * lat_rows)
    grid_vals = lax.dot_general(
        flat, fourier_flat, (((0,), (0,)), ((), ())), preferred_element_type=jnp.float32
    )
    grid_vals = (
        grid_vals.reshape(items * single, lat_rows, fourier_flat.shape[1]) * obs_weight[None, :, :]
    )
    weighted = grid_vals.astype(jnp.bfloat16).reshape(
        items * single * lat_rows, fourier_flat.shape[1]
    )
    returned = lax.dot_general(
        fourier_flat, weighted, (((1,), (1,)), ((), ())), preferred_element_type=jnp.float32
    ).astype(jnp.bfloat16)
    return returned.reshape(slots, parts, items, single, lat_rows)


def legendre_back(returned, legendre):
    return lax.dot_general(
        returned, legendre, (((4,), (2,)), ((0,), (0,))), preferred_element_type=jnp.float32
    )


def paired_sums(residual, image_vec):
    return (
        by_axis(jnp.sum(residual * residual), BAND_FIELD),
        by_axis(jnp.sum(residual * image_vec), BAND_FIELD),
    )


def on_device(right_side, legendre, wave_map, obs_weight):
    slot_count = legendre.shape[0]
    band_count = lax.axis_size(BAND)
    lat_rows = obs_weight.shape[0]
    first_slot = lax.axis_index(BAND) * slot_count
    own_waves = lax.dynamic_slice_in_dim(wave_map, first_slot, slot_count)
    triangle = triangle_of(own_waves, right_side.shape[4])
    fourier_table = fourier_of(wave_map, obs_weight.shape[1])
    fourier_flat = fourier_table.reshape(2 * fourier_table.shape[0], fourier_table.shape[2])
    triangle_five = triangle[:, None, None, None, :]
    field_count = right_side.shape[2]
    level_count = right_side.shape[3]
    merged = field_count * level_count

    def operate(vector):
        masked_bf = (vector * triangle_five).astype(jnp.bfloat16)
        coeffs = lax.dot_general(
            masked_bf, legendre, (((4,), (1,)), ((0,), (0,))), preferred_element_type=jnp.float32
        ).astype(jnp.bfloat16)
        outgoing = coeffs.reshape(slot_count, 2, merged, band_count, lat_rows)
        spread = lax.all_to_all(outgoing, BAND, split_axis=3, concat_axis=0, tiled=True)
        returned = grid_round(spread, fourier_flat, obs_weight)
        returned_home = lax.all_to_all(returned, BAND, split_axis=0, concat_axis=3, tiled=True)
        home = returned_home.reshape(slot_count, 2, field_count, level_count, band_count * lat_rows)
        adjoint = legendre_back(home, legendre)
        return vector + triangle_five * adjoint

    residual = right_side * triangle_five
    solution = jnp.zeros_like(residual)
    image_vec = operate(residual)
    norm_now, product = paired_sums(residual, image_vec)
    step_length = norm_now / product
    direction = residual
    along = image_vec
    for iteration in range(ITERS):
        solution = solution + step_length * direction
        residual = residual - step_length * along
        if iteration + 1 < ITERS:
            image_vec = operate(residual)
            norm_next, product = paired_sums(residual, image_vec)
            beta_ratio = norm_next / norm_now
            step_length = norm_next / (product - beta_ratio * norm_next / step_length)
            direction = residual + beta_ratio * direction
            along = image_vec + beta_ratio * along
            norm_now = norm_next
    return (solution, residual)


def solution(mesh):
    split = Mesh(
        mesh.devices.reshape(8, 4, 2, mesh.shape["field"]), ("band_0", "band_1", "band_2", "field")
    )
    return jax.shard_map(
        on_device,
        mesh=split,
        in_specs=(P(BAND, None, "field", None, None), P(BAND, None, None), P(), P(BAND, None)),
        out_specs=(P(BAND, None, "field", None, None), P(BAND, None, "field", None, None)),
        check_vma=False,
    )
```

profile of v0, /device:TPU:1, one launch (start us, length us, event | category | flops | bytes accessed | tf_op | source)
XLA Modules:
  0.0 736.9 jit_solution(9783474237335254011)
XLA Ops:
  6.4 9.7 %reshape.240 = bf16[10,2,12,64,10]{4,3,2,1,0:T(8,128)(2,1)} reshape(bf16[10,2,12,640]{3,2,1,0:T(8,128)(2,1)S(1)} %fusion.49) | data formatting | bytes 614400 | tf_op jit(solution)/shard_map/reshape | solution.py:83
  16.1 14.1 %copy.117 = bf16[10,2,12,64,10]{2,1,4,0,3:T(2,128)(2,1)S(1)} copy(bf16[10,2,12,64,10]{4,3,2,1,0:T(8,128)(2,1)} %reshape.240) | data formatting | bytes 614400 | tf_op jit(solution)/shard_map/reshape | solution.py:83
  34.6 13.5 %all-to-all-start = ((bf16[64,2,1200]{2,1,0:T(2,128)(2,1)}), bf16[64,2,1200]{2,1,0:T(2,128)(2,1)}, u32[]{:S(2)}, u32[]{:S(2)}) async-start(bf16[64,2,1200]{2,1,0:T(2,128)(2,1)} %reshape.247), calls=%async_computation | async-start | bytes 655360 | tf_op jit(solution)/shard_map/all_to_all | solution.py:84
  48.1 13.8 %fusion.17 = (f32[640,1,1280]{2,0,1:T(8,128)S(1)}, f32[640,1,1280]{2,0,1:T(8,128)S(1)}) fusion(s32[640]{0:T(1024)S(1)} %copy-done.2), kind=kLoop, calls=%fused_computation.21 | loop fusion | flops 8192000 | bytes 6556160 | tf_op jit(solution)/shard_map/cos | solution.py:28
  84.4 13.4 %copy.118 = bf16[64,10,2,12,1,10]{5,3,2,1,0,4:T(8,128)(2,1)} copy(bf16[64,10,2,12,1,10]{3,2,5,1,0,4:T(2,128)(2,1)} %bitcast_bitcast_fusion.2) | data formatting | bytes 614400 | tf_op jit(solution)/shard_map/all_to_all | solution.py:84
  120.9 12.1 %copy.123 = bf16[640,2,12,1,10]{2,1,4,3,0:T(2,128)(2,1)S(1)} copy(bf16[640,2,12,1,10]{4,2,1,0,3:T(8,128)(2,1)} %reshape.224) | data formatting | bytes 614400 | tf_op jit(solution)/shard_map/reshape | solution.py:48
  137.4 24.8 %all_to_all.90 = bf16[64,2,1200]{2,1,0:T(2,128)(2,1)} all-to-all(bf16[64,2,1200]{2,1,0:T(2,128)(2,1)} %reshape.249), channel_id=1, replica_groups=mesh['band_0'=8,'band_1'=4,'band_2'=2,'field'=4] {'band_0','band_1','ban..., dimensions={0} | all-to-all | bytes 614400 | tf_op jit(solution)/shard_map/all_to_all | solution.py:86
  170.0 17.5 %copy.154 = bf16[64,10,2,12,1,10]{1,0,2,5,3,4:T(8,128)(2,1)} copy(bf16[64,10,2,12,1,10]{3,2,5,1,0,4:T(2,128)(2,1)S(1)} %bitcast.136) | data formatting | bytes 614400 | tf_op jit(solution)/shard_map/all_to_all | solution.py:86
  187.5 12.6 %copy.155 = bf16[10,2,12,64,1,10]{5,3,2,1,0,4:T(8,128)(2,1)} copy(bf16[10,2,12,64,1,10]{0,3,1,5,2,4:T(8,128)(2,1)} %bitcast.132) | data formatting | bytes 614400 | tf_op jit(solution)/shard_map/reshape.6
  213.3 12.5 %all-reduce.2 = (f32[]{:T(128)}, f32[]{:T(128)}) all-reduce(f32[]{:T(128)} %get-tuple-element.17, f32[]{:T(128)} %get-tuple-element.16), channel_id=1, replica_groups=mesh['band_0'=8,'band_1'=4,'band_2'=2,'field'=4] {'band_0'}, use_global_device_ids=true, to_apply=%region_1.2 | all-reduce | flops 2 | bytes 16 | tf_op jit(solution)/shard_map/psum | solution.py:16
  233.1 9.4 %all-reduce.11 = (f32[]{:T(128)}, f32[]{:T(128)}) all-reduce(f32[]{:T(128)} %get-tuple-element.34, f32[]{:T(128)} %get-tuple-element.35), channel_id=1, replica_groups=mesh['band_0'=8,'band_1'=4,'band_2'=2,'field'=4] {'band_2'}, use_global_device_ids=true, to_apply=%region_3.4 | all-reduce | flops 2 | bytes 16 | tf_op jit(solution)/shard_map/psum | solution.py:16
  242.5 9.4 %all-reduce.5 = (f32[]{:T(128)}, f32[]{:T(128)}) all-reduce(f32[]{:T(128)} %get-tuple-element.40, f32[]{:T(128)} %get-tuple-element.41), channel_id=1, replica_groups=mesh['band_0'=8,'band_1'=4,'band_2'=2,'field'=4] {'field'}, use_global_device_ids=true, to_apply=%region_4.5 | all-reduce | flops 2 | bytes 16 | tf_op jit(solution)/shard_map/psum | solution.py:16
  258.0 9.7 %reshape.243 = bf16[10,2,12,64,10]{4,3,2,1,0:T(8,128)(2,1)} reshape(bf16[10,2,12,640]{3,2,1,0:T(8,128)(2,1)S(1)} %fusion.52) | data formatting | bytes 614400 | tf_op jit(solution)/shard_map/reshape | solution.py:83
  267.8 14.6 %copy.128 = bf16[10,2,12,64,10]{2,1,4,0,3:T(2,128)(2,1)} copy(bf16[10,2,12,64,10]{4,3,2,1,0:T(8,128)(2,1)} %reshape.243) | data formatting | bytes 614400 | tf_op jit(solution)/shard_map/reshape | solution.py:83
  289.3 22.1 %all_to_all.91 = bf16[64,2,1200]{2,1,0:T(2,128)(2,1)S(1)} all-to-all(bf16[64,2,1200]{2,1,0:T(2,128)(2,1)S(1)} %reshape.251), channel_id=1, replica_groups=mesh['band_0'=8,'band_1'=4,'band_2'=2,'field'=4] {'band_0','band_1','ban..., dimensions={0} | all-to-all | bytes 614400 | tf_op jit(solution)/shard_map/all_to_all | solution.py:84
  321.3 13.2 %copy.129 = bf16[64,10,2,12,1,10]{5,3,2,1,0,4:T(8,128)(2,1)} copy(bf16[64,10,2,12,1,10]{3,2,5,1,0,4:T(2,128)(2,1)} %bitcast_bitcast_fusion.1) | data formatting | bytes 614400 | tf_op jit(solution)/shard_map/all_to_all | solution.py:84
  355.7 12.7 %copy.134 = bf16[640,2,12,1,10]{2,1,4,3,0:T(2,128)(2,1)} copy(bf16[640,2,12,1,10]{4,2,1,0,3:T(8,128)(2,1)} %reshape.230) | data formatting | bytes 614400 | tf_op jit(solution)/shard_map/reshape | solution.py:48
  375.4 19.2 %all_to_all.92 = bf16[64,2,1200]{2,1,0:T(2,128)(2,1)S(1)} all-to-all(bf16[64,2,1200]{2,1,0:T(2,128)(2,1)S(1)} %reshape.253), channel_id=1, replica_groups=mesh['band_0'=8,'band_1'=4,'band_2'=2,'field'=4] {'band_0','band_1','ban..., dimensions={0} | all-to-all | bytes 614400 | tf_op jit(solution)/shard_map/all_to_all | solution.py:86
  398.5 15.4 %copy.158 = bf16[64,10,2,12,1,10]{1,0,2,5,3,4:T(8,128)(2,1)} copy(bf16[64,10,2,12,1,10]{3,2,5,1,0,4:T(2,128)(2,1)} %bitcast.138) | data formatting | bytes 614400 | tf_op jit(solution)/shard_map/all_to_all | solution.py:86
  413.9 12.6 %copy.159 = bf16[10,2,12,64,1,10]{5,3,2,1,0,4:T(8,128)(2,1)} copy(bf16[10,2,12,64,1,10]{0,3,1,5,2,4:T(8,128)(2,1)} %bitcast.133) | data formatting | bytes 614400 | tf_op jit(solution)/shard_map/reshape.12
  440.6 12.5 %all-reduce.1 = (f32[]{:T(128)}, f32[]{:T(128)}) all-reduce(f32[]{:T(128)} %get-tuple-element.15, f32[]{:T(128)} %get-tuple-element.14), channel_id=1, replica_groups=mesh['band_0'=8,'band_1'=4,'band_2'=2,'field'=4] {'band_0'}, use_global_device_ids=true, to_apply=%region_11.12 | all-reduce | flops 2 | bytes 16 | tf_op jit(solution)/shard_map/psum | solution.py:16
  460.5 9.5 %all-reduce.10 = (f32[]{:T(128)}, f32[]{:T(128)}) all-reduce(f32[]{:T(128)} %get-tuple-element.32, f32[]{:T(128)} %get-tuple-element.33), channel_id=1, replica_groups=mesh['band_0'=8,'band_1'=4,'band_2'=2,'field'=4] {'band_2'}, use_global_device_ids=true, to_apply=%region_13.14 | all-reduce | flops 2 | bytes 16 | tf_op jit(solution)/shard_map/psum | solution.py:16
  488.0 10.4 %reshape.245 = bf16[10,2,12,64,10]{4,3,2,1,0:T(8,128)(2,1)} reshape(bf16[10,2,12,640]{3,2,1,0:T(8,128)(2,1)} %fusion.55) | data formatting | bytes 614400 | tf_op jit(solution)/shard_map/reshape | solution.py:83
  498.4 14.6 %copy.139 = bf16[10,2,12,64,10]{2,1,4,0,3:T(2,128)(2,1)} copy(bf16[10,2,12,64,10]{4,3,2,1,0:T(8,128)(2,1)} %reshape.245) | data formatting | bytes 614400 | tf_op jit(solution)/shard_map/reshape | solution.py:83
  520.6 21.8 %all_to_all.93 = bf16[64,2,1200]{2,1,0:T(2,128)(2,1)} all-to-all(bf16[64,2,1200]{2,1,0:T(2,128)(2,1)} %reshape.255), channel_id=1, replica_groups=mesh['band_0'=8,'band_1'=4,'band_2'=2,'field'=4] {'band_0','band_1','ban..., dimensions={0} | all-to-all | bytes 614400 | tf_op jit(solution)/shard_map/all_to_all | solution.py:84
  556.9 13.2 %copy.140 = bf16[64,10,2,12,1,10]{5,3,2,1,0,4:T(8,128)(2,1)} copy(bf16[64,10,2,12,1,10]{3,2,5,1,0,4:T(2,128)(2,1)} %bitcast_bitcast_fusion) | data formatting | bytes 614400 | tf_op jit(solution)/shard_map/all_to_all | solution.py:84
  598.8 12.7 %copy.145 = bf16[640,2,12,1,10]{2,1,4,3,0:T(2,128)(2,1)} copy(bf16[640,2,12,1,10]{4,2,1,0,3:T(8,128)(2,1)} %reshape.236) | data formatting | bytes 614400 | tf_op jit(solution)/shard_map/reshape | solution.py:48
  619.1 19.6 %all_to_all.94 = bf16[64,2,1200]{2,1,0:T(2,128)(2,1)} all-to-all(bf16[64,2,1200]{2,1,0:T(2,128)(2,1)} %reshape.257), channel_id=1, replica_groups=mesh['band_0'=8,'band_1'=4,'band_2'=2,'field'=4] {'band_0','band_1','ban..., dimensions={0} | all-to-all | bytes 614400 | tf_op jit(solution)/shard_map/all_to_all | solution.py:86
  647.3 15.4 %copy.162 = bf16[64,10,2,12,1,10]{1,0,2,5,3,4:T(8,128)(2,1)} copy(bf16[64,10,2,12,1,10]{3,2,5,1,0,4:T(2,128)(2,1)} %bitcast.140) | data formatting | bytes 614400 | tf_op jit(solution)/shard_map/all_to_all | solution.py:86
  662.8 12.7 %copy.163 = bf16[10,2,12,64,1,10]{5,3,2,1,0,4:T(8,128)(2,1)} copy(bf16[10,2,12,64,1,10]{0,3,1,5,2,4:T(8,128)(2,1)} %bitcast.134) | data formatting | bytes 614400 | tf_op jit(solution)/shard_map/reshape.18
  690.2 12.5 %all-reduce = (f32[]{:T(128)}, f32[]{:T(128)}) all-reduce(f32[]{:T(128)} %get-tuple-element.13, f32[]{:T(128)} %get-tuple-element.12), channel_id=1, replica_groups=mesh['band_0'=8,'band_1'=4,'band_2'=2,'field'=4] {'band_0'}, use_global_device_ids=true, to_apply=%region_21.22 | all-reduce | flops 2 | bytes 16 | tf_op jit(solution)/shard_map/psum | solution.py:16
  710.0 9.4 %all-reduce.9 = (f32[]{:T(128)}, f32[]{:T(128)}) all-reduce(f32[]{:T(128)} %get-tuple-element.30, f32[]{:T(128)} %get-tuple-element.31), channel_id=1, replica_groups=mesh['band_0'=8,'band_1'=4,'band_2'=2,'field'=4] {'band_2'}, use_global_device_ids=true, to_apply=%region_23.24 | all-reduce | flops 2 | bytes 16 | tf_op jit(solution)/shard_map/psum | solution.py:16
  (76 shorter events, 279.2 us)
Async XLA Ops:
  30.2 17.9 %copy-start.2 = (s32[640]{0:T(1024)S(1)}, s32[640]{0:T(1024)}, u32[]{:S(2)}) copy-start(s32[640]{0:T(1024)} %param.6) | copy-start | bytes 7684
  34.6 38.0 %all-to-all-start = ((bf16[64,2,1200]{2,1,0:T(2,128)(2,1)}), bf16[64,2,1200]{2,1,0:T(2,128)(2,1)}, u32[]{:S(2)}, u32[]{:S(2)}) async-start(bf16[64,2,1200]{2,1,0:T(2,128)(2,1)} %reshape.247), calls=%async_computation | async-start | bytes 655360 | tf_op jit(solution)/shard_map/all_to_all | solution.py:84
  97.8 7.5 %copy-start.3 = (f32[10,1280]{1,0:T(8,128)S(1)}, f32[10,1280]{1,0:T(8,128)}, u32[]{:S(2)}) copy-start(f32[10,1280]{1,0:T(8,128)} %param.7) | copy-start | bytes 153604
  105.3 5.7 copy-start.1
  200.1 6.7 copy-start
where the time goes:
time: 747 us; the launch traced here: 737 us
  local copies, waits for them, and re-layouts  419 us (56%)
  blocking collectives  219 us (29%)
  matrix products  55.6 us (7%)
  other arithmetic  18 us (2%)
  starting transfers between devices  13.5 us (2%)
  between operations  11.1 us (1%)
    psum x12, blocking collectives, by_axis(): return functools.reduce(lax.psum, axes, array)  112 us
    unnamed x22, local copies, waits for them, and re-layouts  81.6 us
    reshape x6, local copies, waits for them, and re-layouts, operate(): outgoing = coeffs.reshape(slot_count, 2, merged, band_count, lat_rows)  73.1 us
    all_to_all x3, blocking collectives, operate(): lax.all_to_all(returned, BAND, split_axis=0, concat_axis=3, tiled=True)  63.6 us
    another operation x6, local copies, waits for them, and re-layouts  58.5 us
    all_to_all x6, local copies, waits for them, and re-layouts, operate(): lax.all_to_all(outgoing, BAND, split_axis=3, concat_axis=0, tiled=True)  55.7 us
    reshape x6, local copies, waits for them, and re-layouts, grid_round(): return returned.reshape(slots, parts, items, single, lat_rows)  55.6 us
    all_to_all x3, local copies, waits for them, and re-layouts, operate(): lax.all_to_all(returned, BAND, split_axis=0, concat_axis=3, tiled=True)  48.3 us
  transfers between devices with their start and end apart: 1, of which 0 were waited for; matrix products, arithmetic and copies ran while one was open for 3% of the time, Pallas kernels for 0%

commit v1 on v0

v1 whole, which is shorter than its diff:
```python
import math

import jax
import jax.numpy as jnp
import numpy as np
from jax import lax
from jax.experimental import pallas as pl
from jax.experimental.pallas import tpu as pltpu
from jax.sharding import PartitionSpec as P

ITERS = 3
BANDS = 64
FIELD = 4
SLOTS = 10
LEV = 12
MW = 640
NLON = 1280
LANES = 128
LATBLOCKS = 5
WORKERS = LEV * LATBLOCKS
MSG = 2 * SLOTS
OWN_ROWS = SLOTS * 2 * LEV * LATBLOCKS
HALF = NLON // 2
KPAD = 656
WCOL = 704
WROW = 16
WSRC = 14
MESH = pl.DeviceIdType.MESH


def small_tables():
    k = np.arange(KPAD)
    keep = (k <= HALF).astype(np.float64)
    out = []
    for count, step in ((MW // 32, 32), (32, 1)):
        phase = (np.arange(count)[:, None] * step * k[None, :]) % NLON
        angle = phase * (2.0 * math.pi / NLON)
        out.append((np.cos(angle) * keep).astype(np.float32))
        out.append((np.sin(angle) * keep).astype(np.float32))
    return out


def spread_offset(i):
    half = lax.div(i + 1, 2)
    return jnp.where(lax.rem(i, 2) == 1, half, BANDS - half)


def kernel(
    rhs, leg_hbm, tri, wave_row, wts, ca, sa, cb, sb,
    x_ref, r_ref,
    leg, p_ref, s_ref, z_ref, stage, fsend, frecv, gsend, grecv,
    tc, ts, ckm, skm, cmk, smk, wa, wb, wrecv, a1s, a1r, a2s, a2r, scal,
    leg_sem, f_ssem, f_rsem, g_ssem, g_rsem, w_ssem, w_rsem, a1_ssem, a1_rsem, a2_ssem, a2_rsem,
):
    me = lax.axis_index("band")
    fld = lax.axis_index("field")
    zz = lax.div(me, 8)
    yy = lax.rem(lax.div(me, 2), 4)
    core = lax.rem(me, 2)
    worker = me < WORKERS

    wrecv[pl.ds((WSRC - 1) * WROW, WROW), :] = jnp.zeros((WROW, 2 * WCOL), jnp.bfloat16)

    barrier = pltpu.get_barrier_semaphore()

    def greet_band(i, c):
        pl.semaphore_signal(barrier, inc=1, device_id={"band": lax.rem(me + i, BANDS)}, device_id_type=MESH)
        return c

    def greet_field(i, c):
        f2 = lax.rem(fld + 1 + lax.div(i, 4), FIELD)
        b2 = zz * 8 + lax.rem(i, 4) * 2 + core
        pl.semaphore_signal(barrier, inc=1, device_id={"band": b2, "field": f2}, device_id_type=MESH)
        return c

    lax.fori_loop(1, BANDS, greet_band, 0)
    lax.fori_loop(0, 12, greet_field, 0)

    def leg_copy(s):
        return pltpu.make_async_copy(leg_hbm.at[s], leg.at[s], leg_sem.at[s])

    def start_leg(s, c):
        leg_copy(s).start()
        return c

    lax.fori_loop(0, SLOTS, start_leg, 0)

    def mask_slot(s, c):
        for j in range(LATBLOCKS):
            rows = pl.ds(s * 120 + j, 24, stride=5)
            r_ref[rows, :] = rhs[rows, :] * tri[s, :, 128 * j : 128 * j + 128]
        return c

    lax.fori_loop(0, SLOTS, mask_slot, 0)
    r0 = r_ref[...]
    scal[0:1, :] = jnp.sum(r0 * r0, axis=0, keepdims=True)
    scal[1:2, :] = jnp.ones((1, LANES), jnp.float32)
    scal[2:3, :] = jnp.ones((1, LANES), jnp.float32)
    x_ref[...] = jnp.zeros_like(r0)
    p_ref[...] = jnp.zeros_like(r0)
    s_ref[...] = jnp.zeros_like(r0)

    pl.semaphore_wait(barrier, BANDS - 1 + 12)

    lat0 = me * SLOTS
    blk_lo = lax.div(lat0, LANES)
    blk_hi = lax.div(lat0 + SLOTS - 1, LANES)

    def first_src(j):
        return lax.div(j * LANES, SLOTS)

    def w_dst(j):
        return wrecv.at[pl.ds((me - first_src(j)) * WROW, WROW)]

    def send_weights(j):
        def one(i, c):
            g = j * LEV + i

            @pl.when(g != me)
            def _():
                pltpu.make_async_remote_copy(
                    wts, w_dst(j), w_ssem, w_rsem, device_id={"band": g}, device_id_type=MESH
                ).start()

            @pl.when(g == me)
            def _():
                pltpu.make_async_copy(wts, w_dst(j), w_rsem).start()

            return c

        lax.fori_loop(0, LEV, one, 0)

    send_weights(blk_lo)

    @pl.when(blk_hi != blk_lo)
    def _():
        send_weights(blk_hi)

    my_block = lax.div(me, LEV)

    def iteration(it, carry):
        def forward(s, c):
            @pl.when(it == 0)
            def _():
                leg_copy(s).wait()

            base = s * 120
            vec = jnp.concatenate(
                [r_ref[pl.ds(base + j, 24, stride=5), :] for j in range(LATBLOCKS)], axis=1
            ).astype(jnp.bfloat16)
            out = jnp.dot(vec, leg[s], preferred_element_type=jnp.float32)
            for j in range(LATBLOCKS):
                for cc in range(2):
                    stage[pl.ds(j * 240 + 2 * s + cc, LEV, stride=MSG), :] = out[
                        LEV * cc : LEV * cc + LEV, 128 * j : 128 * j + 128
                    ]
            return c

        lax.fori_loop(0, SLOTS, forward, 0)
        fsend[...] = stage[0:OWN_ROWS, :].astype(jnp.bfloat16)

        def f_block(g):
            return fsend.at[pl.ds(pl.multiple_of(g * MSG, 4), MSG)]

        f_dst = frecv.at[it, pl.ds(pl.multiple_of(me * MSG, 4), MSG)]

        @pl.when(worker)
        def _():
            pltpu.make_async_copy(f_block(me), f_dst, f_rsem.at[it]).start()

        def f_go(i, c):
            g = lax.rem(me + spread_offset(i), BANDS)

            @pl.when(g < WORKERS)
            def _():
                pltpu.make_async_remote_copy(
                    f_block(g), f_dst, f_ssem, f_rsem.at[it], device_id={"band": g}, device_id_type=MESH
                ).start()

            return c

        lax.fori_loop(1, BANDS, f_go, 0)

        @pl.when(it == 0)
        def _():
            norm = 1.0 / math.sqrt(MW)
            for a in range(MW // 32):
                cosa, sina = ca[a : a + 1, :], sa[a : a + 1, :]
                tc[32 * a : 32 * a + 32, :] = ((cosa * cb[...] - sina * sb[...]) * norm).astype(jnp.bfloat16)
                ts[32 * a : 32 * a + 32, :] = ((sina * cb[...] + cosa * sb[...]) * -norm).astype(jnp.bfloat16)
            pick = (
                lax.broadcasted_iota(jnp.int32, (MW, MW), 0) == wave_row[...]
            ).astype(jnp.float32).astype(jnp.bfloat16)
            contract = (((0,), (0,)), ((), ()))
            for src, km, mk in ((tc, ckm, cmk), (ts, skm, smk)):
                km[...] = lax.dot_general(
                    src[...], pick, contract, preferred_element_type=jnp.float32
                ).astype(jnp.bfloat16)
                mk[...] = lax.dot_general(
                    pick, src[...], contract, preferred_element_type=jnp.float32
                ).astype(jnp.bfloat16)

        @pl.when(jnp.logical_and(it == 0, worker))
        def _():
            edge = jnp.logical_or(my_block == 0, my_block == LATBLOCKS - 1)

            @pl.when(edge)
            def _():
                part13 = wrecv.at[pl.ds(0, 13 * WROW)]
                pltpu.make_async_copy(part13, part13, w_rsem).wait()

            @pl.when(jnp.logical_not(edge))
            def _():
                pltpu.make_async_copy(wrecv, wrecv, w_rsem).wait()

            row = lax.broadcasted_iota(jnp.int32, (WSRC * WROW, LANES), 0)
            lat = lax.broadcasted_iota(jnp.int32, (WSRC * WROW, LANES), 1)
            src_lat = (first_src(my_block) + row // WROW) * SLOTS + row % WROW
            hit = jnp.logical_and(row % WROW < SLOTS, src_lat - my_block * LANES == lat)
            spot = hit.astype(jnp.float32).astype(jnp.bfloat16)
            turned = lax.dot_general(
                wrecv[...], spot, (((0,), (0,)), ((), ())), preferred_element_type=jnp.float32
            )
            wa[...] = turned[0:KPAD]
            wb[...] = turned[WCOL : WCOL + KPAD]

        scal[3:4, :] = jnp.zeros((1, LANES), jnp.float32)

        @pl.when(worker)
        def _():
            pltpu.make_async_copy(frecv.at[it], frecv.at[it], f_rsem.at[it]).wait()
            stage[...] = frecv[it].astype(jnp.float32)
            even_in = stage[pl.ds(0, MW, stride=2), :].astype(jnp.bfloat16)
            odd_in = stage[pl.ds(1, MW, stride=2), :].astype(jnp.bfloat16)
            cg = jnp.dot(ckm[...], even_in, preferred_element_type=jnp.float32)
            sg = jnp.dot(skm[...], odd_in, preferred_element_type=jnp.float32)
            even = wa[...] * cg + wb[...] * sg
            odd = wb[...] * cg + wa[...] * sg
            scal[3:4, :] = jnp.sum(cg * even + sg * odd, axis=0, keepdims=True)
            stage[pl.ds(0, MW, stride=2), :] = jnp.dot(
                cmk[...], even.astype(jnp.bfloat16), preferred_element_type=jnp.float32
            )
            stage[pl.ds(1, MW, stride=2), :] = jnp.dot(
                smk[...], odd.astype(jnp.bfloat16), preferred_element_type=jnp.float32
            )
            gsend[...] = stage[...].astype(jnp.bfloat16)

            def g_block(d):
                return gsend.at[pl.ds(pl.multiple_of(d * MSG, 4), MSG)]

            g_dst = grecv.at[it, pl.ds(pl.multiple_of(me * MSG, 4), MSG)]
            pltpu.make_async_copy(g_block(me), g_dst, g_rsem.at[it]).start()

            def g_go(i, c):
                d = lax.rem(me + spread_offset(i), BANDS)
                pltpu.make_async_remote_copy(
                    g_block(d), g_dst, g_ssem, g_rsem.at[it], device_id={"band": d}, device_id_type=MESH
                ).start()
                return c

            lax.fori_loop(1, BANDS, g_go, 0)

        pair = jnp.concatenate([scal[0:1, :], scal[3:4, :]], axis=0)
        own1 = zz * 2 + core
        own2 = fld * 4 + yy
        a1s[it] = pair
        a1r[it, own1] = pair

        def a1_go(i, c):
            o = lax.rem(own1 + i, 16)
            b2 = lax.div(o, 2) * 8 + yy * 2 + lax.rem(o, 2)
            pltpu.make_async_remote_copy(
                a1s.at[it], a1r.at[it, own1], a1_ssem.at[it], a1_rsem.at[it],
                device_id={"band": b2}, device_id_type=MESH,
            ).start()
            return c

        lax.fori_loop(1, 16, a1_go, 0)
        fifteen1 = a1r.at[it, pl.ds(0, 15)]
        pltpu.make_async_copy(fifteen1, fifteen1, a1_rsem.at[it]).wait()
        total1 = jnp.sum(a1r[it], axis=0)
        a2s[it] = total1
        a2r[it, own2] = total1

        def a2_go(i, c):
            o = lax.rem(own2 + i, 16)
            b2 = zz * 8 + lax.rem(o, 4) * 2 + core
            pltpu.make_async_remote_copy(
                a2s.at[it], a2r.at[it, own2], a2_ssem.at[it], a2_rsem.at[it],
                device_id={"band": b2, "field": lax.div(o, 4)}, device_id_type=MESH,
            ).start()
            return c

        lax.fori_loop(1, 16, a2_go, 0)

        pltpu.make_async_copy(grecv.at[it], grecv.at[it], g_rsem.at[it]).wait()
        stage[0:OWN_ROWS, :] = grecv[it].astype(jnp.float32)

        def backward(s, c):
            vec = jnp.concatenate(
                [
                    jnp.concatenate(
                        [stage[pl.ds(j * 240 + 2 * s + cc, LEV, stride=MSG), :] for cc in range(2)], axis=0
                    )
                    for j in range(LATBLOCKS)
                ],
                axis=1,
            ).astype(jnp.bfloat16)
            out = lax.dot_general(
                vec, leg[s], (((1,), (1,)), ((), ())), preferred_element_type=jnp.float32
            )
            out = out * tri[s]
            base = s * 120
            for j in range(LATBLOCKS):
                rows = pl.ds(base + j, 24, stride=5)
                z_ref[rows, :] = r_ref[rows, :] + out[:, 128 * j : 128 * j + 128]
            return c

        lax.fori_loop(0, SLOTS, backward, 0)

        fifteen2 = a2r.at[it, pl.ds(0, 15)]
        pltpu.make_async_copy(fifteen2, fifteen2, a2_rsem.at[it]).wait()
        total2 = jnp.sum(jnp.sum(a2r[it], axis=0), axis=1, keepdims=True)
        rr = jnp.broadcast_to(total2[0:1, :], (1, LANES))
        product = jnp.broadcast_to(total2[0:1, :] + total2[1:2, :], (1, LANES))
        first = jnp.where(it == 0, 0.0, 1.0)
        beta = rr / scal[1:2, :] * first
        alpha = rr / (product - beta * rr / scal[2:3, :])
        scal[1:2, :] = rr
        scal[2:3, :] = alpha
        residual = r_ref[...]
        direction = residual + beta * p_ref[...]
        along = z_ref[...] + beta * s_ref[...]
        p_ref[...] = direction
        s_ref[...] = along
        x_ref[...] = x_ref[...] + alpha * direction
        residual = residual - alpha * along
        r_ref[...] = residual
        scal[0:1, :] = jnp.sum(residual * residual, axis=0, keepdims=True)

        most = frecv.at[0, pl.ds(0, 59 * MSG)]

        @pl.when(worker)
        def _():
            pltpu.make_async_copy(most, most, f_ssem).wait()
            sent = gsend.at[pl.ds(0, 63 * MSG)]
            pltpu.make_async_copy(sent, sent, g_ssem).wait()

        @pl.when(jnp.logical_not(worker))
        def _():
            sent = frecv.at[0, pl.ds(0, 60 * MSG)]
            pltpu.make_async_copy(sent, sent, f_ssem).wait()

        pltpu.make_async_copy(fifteen1, fifteen1, a1_ssem.at[it]).wait()
        pltpu.make_async_copy(fifteen2, fifteen2, a2_ssem.at[it]).wait()
        return carry

    lax.fori_loop(0, ITERS, iteration, 0)

    def w_sent(j):
        mine = jnp.logical_and(j * LEV <= me, me < j * LEV + LEV)

        @pl.when(mine)
        def _():
            part_ref = wrecv.at[pl.ds(0, 11 * WROW)]
            pltpu.make_async_copy(part_ref, part_ref, w_ssem).wait()

        @pl.when(jnp.logical_not(mine))
        def _():
            part_ref = wrecv.at[pl.ds(0, 12 * WROW)]
            pltpu.make_async_copy(part_ref, part_ref, w_ssem).wait()

    w_sent(blk_lo)

    @pl.when(blk_hi != blk_lo)
    def _():
        w_sent(blk_hi)


def on_device(right_side, legendre, wave_map, obs_weight):
    first_slot = lax.axis_index("band") * SLOTS
    own_waves = lax.dynamic_slice_in_dim(wave_map, first_slot, SLOTS)
    tri = (jnp.arange(MW, dtype=jnp.int32)[None, :] >= own_waves[:, None]).astype(jnp.float32)
    plus = obs_weight[:, : HALF + 1]
    mirror = jnp.pad(obs_weight[:, : HALF : -1], ((0, 0), (1, 1)))
    pad = ((0, WROW - SLOTS), (0, WCOL - HALF - 1))
    wts = jnp.concatenate([jnp.pad(plus + mirror, pad), jnp.pad(plus - mirror, pad)], axis=1).astype(jnp.bfloat16)
    tables = [jnp.asarray(t) for t in small_tables()]
    vmem = pl.BlockSpec(memory_space=pltpu.VMEM)
    f32, bf16 = jnp.float32, jnp.bfloat16
    dma = pltpu.SemaphoreType.DMA
    shape = jax.ShapeDtypeStruct((OWN_ROWS, LANES), f32)
    x, r = pl.pallas_call(
        kernel,
        out_shape=(shape, shape),
        in_specs=[vmem, pl.BlockSpec(memory_space=pl.ANY)] + [vmem] * 7,
        out_specs=(vmem, vmem),
        scratch_shapes=[
            pltpu.VMEM((SLOTS, MW, MW), bf16),
            pltpu.VMEM((OWN_ROWS, LANES), f32),
            pltpu.VMEM((OWN_ROWS, LANES), f32),
            pltpu.VMEM((OWN_ROWS, LANES), f32),
            pltpu.VMEM((BANDS * MSG, LANES), f32),
            pltpu.VMEM((OWN_ROWS, LANES), bf16),
            pltpu.VMEM((ITERS, BANDS * MSG, LANES), bf16),
            pltpu.VMEM((BANDS * MSG, LANES), bf16),
            pltpu.VMEM((ITERS, OWN_ROWS, LANES), bf16),
            pltpu.VMEM((MW, KPAD), bf16),
            pltpu.VMEM((MW, KPAD), bf16),
            pltpu.VMEM((KPAD, MW), bf16),
            pltpu.VMEM((KPAD, MW), bf16),
            pltpu.VMEM((MW, KPAD), bf16),
            pltpu.VMEM((MW, KPAD), bf16),
            pltpu.VMEM((KPAD, LANES), f32),
            pltpu.VMEM((KPAD, LANES), f32),
            pltpu.VMEM((WSRC * WROW, 2 * WCOL), bf16),
            pltpu.VMEM((ITERS, 2, LANES), f32),
            pltpu.VMEM((ITERS, 16, 2, LANES), f32),
            pltpu.VMEM((ITERS, 2, LANES), f32),
            pltpu.VMEM((ITERS, 16, 2, LANES), f32),
            pltpu.VMEM((8, LANES), f32),
            dma((SLOTS,)), dma(()), dma((ITERS,)), dma(()), dma((ITERS,)), dma(()), dma(()),
            dma((ITERS,)), dma((ITERS,)), dma((ITERS,)), dma((ITERS,)),
        ],
        compiler_params=pltpu.CompilerParams(
            collective_id=0, has_side_effects=True, vmem_limit_bytes=60 * 1024 * 1024
        ),
    )(
        right_side.reshape(OWN_ROWS, LANES), legendre, tri.reshape(SLOTS, 1, MW), wave_map.reshape(1, MW), wts, *tables
    )
    return x.reshape(right_side.shape), r.reshape(right_side.shape)


def solution(mesh):
    spec = P("band", None, "field", None, None)
    return jax.shard_map(
        on_device,
        mesh=mesh,
        in_specs=(spec, P("band", None, None), P(), P("band", None)),
        out_specs=(spec, spec),
        check_vma=False,
    )
```

time: 747 us -> 129 us (0.17); the launches traced: 737 us -> 129 us
  local copies, waits for them, and re-layouts: 419 us -> 7.96 us
  blocking collectives: 219 us -> 0 us
  Pallas kernels: 0 us -> 118 us
  matrix products: 55.6 us -> 0 us
  other arithmetic: 18 us -> 2.29 us
  starting transfers between devices: 13.5 us -> 0 us
  between operations: 11.1 us -> 0.65 us
    reshape x18 -> x1, local copies, waits for them, and re-layouts: 152 us -> 1.28 us  [on_device(): wave_map.reshape(1, MW)]
    pallas_call x0 -> x1, Pallas kernels: none -> 118 us  [on_device(): pl.pallas_call(kernel, out_shape=(shape, shape), in_specs=[vmem, pl.Block...]
    psum x12 -> x0, blocking collectives: 112 us -> none  [by_axis(): return functools.reduce(lax.psum, axes, array)]
    all_to_all x5 -> x0, blocking collectives: 108 us -> none  [the longest x3 63.6 us: operate(): lax.all_to_all(returned, BAND, split_axis=0, concat_axis=3, tiled=True)]
    all_to_all x9 -> x0, local copies, waits for them, and re-layouts: 104 us -> none  [the longest x6 55.7 us: operate(): lax.all_to_all(outgoing, BAND, split_axis=3, concat_axis=0, tiled=True)]
    unnamed x22 -> x4, local copies, waits for them, and re-layouts: 81.6 us -> 5.07 us
    another operation x6 -> x0, local copies, waits for them, and re-layouts: 58.5 us -> none
    dot_general x12 -> x0, matrix products: 55.6 us -> none  [the longest x3 21.5 us: legendre_back(): lax.dot_general(returned, legendre, (((4,), (2,)), ((0,), (0,))), preferr...]
  transfers between devices with their start and end apart: 1 -> 0, of which waited for: 0 -> 0; matrix products, arithmetic and copies ran while one was open for 3% -> 0% of each run, Pallas kernels for 0% -> 0%
where the time goes in v1:
time: 129 us
  Pallas kernels  118 us (91%)
  local copies, waits for them, and re-layouts  7.96 us (6%)
  other arithmetic  2.29 us (2%)
    pallas_call x1, Pallas kernels, on_device(): pl.pallas_call(kernel, out_shape=(shape, shape), in_specs=[vmem, pl.Block...  118 us
    unnamed x4, local copies, waits for them, and re-layouts  5.07 us

profile of v1, /device:TPU:1, one launch (start us, length us, event | category | flops | bytes accessed | tf_op | source)
XLA Modules:
  0.0 128.7 jit_solution(562160530913127505)
XLA Ops:
  0.6 0.8 dynamic_slice.3
  1.4 1.3 reshape.48.wave_row
  2.7 0.7 compare_convert_fusion.tri
  3.4 0.9 slice.7
  4.2 0.4 reverse
  4.6 0.1 slice.10
  4.7 0.9 fusion.2
  5.6 0.7 fusion.4.wts
  6.3 117.8 %shard_map.95 = (f32[1200,128]{1,0:T(8,128)}, f32[1200,128]{1,0:T(8,128)}) custom-call(f32[1200,128]{1,0:T(8,128)} %bitcast.6, bf16[10,640,640]{2,1,0:T(8,128)(2,1)} %leg_hbm.1, f32[10,1,640]{2,1,0:T(1,128)} %compare_convert_fusion.tri, s32[1,640]{1,0:T(1,128)} %reshape.48.wave_row, bf16[16,1408]{1,0:T(8,128)(2,1)} %fusion.4.wts, ...), custom_call_target="tpu_custom_call" | custom-call | tf_op jit(solution)/shard_map/pallas_call | solution.py:393
  124.1 2.3 %copy.16 = f32[10,2,1,12,640]{4,2,3,1,0:T(1,128)} copy(f32[10,2,1,12,640]{4,2,3,1,0:T(1,128)} %bitcast.5) | data formatting | bytes 1228800
  126.4 2.3 %copy.17 = f32[10,2,1,12,640]{4,2,3,1,0:T(1,128)} copy(f32[10,2,1,12,640]{4,2,3,1,0:T(1,128)} %bitcast.4) | data formatting | bytes 1228800

commit v2 on v1

--- a/solution.py
+++ b/solution.py
@@ -22,7 +22,6 @@
 OWN_ROWS = SLOTS * 2 * LEV * LATBLOCKS
 HALF = NLON // 2
 KPAD = 656
-WCOL = 704
 WROW = 16
 WSRC = 14
 MESH = pl.DeviceIdType.MESH
@@ -40,16 +39,19 @@
     return out
 
 
-def spread_offset(i):
-    half = lax.div(i + 1, 2)
-    return jnp.where(lax.rem(i, 2) == 1, half, BANDS - half)
+def peer(i, zz, yy, core):
+    zi, w = lax.div(i, 8), lax.rem(i, 8)
+    yi = lax.div(w, 2)
+    dz = jnp.where(lax.rem(zi, 2) == 0, 4 + lax.div(zi, 2), 4 - lax.div(zi + 1, 2))
+    dy = jnp.where(lax.rem(yi, 2) == 0, 2 + lax.div(yi, 2), 2 - lax.div(yi + 1, 2))
+    return lax.rem(zz + dz, 8) * 8 + lax.rem(yy + dy, 4) * 2 + lax.rem(core + lax.rem(w, 2), 2)
 
 
 def kernel(
-    rhs, leg_hbm, tri, wave_row, wts, ca, sa, cb, sb,
-    x_ref, r_ref,
-    leg, p_ref, s_ref, z_ref, stage, fsend, frecv, gsend, grecv,
-    tc, ts, ckm, skm, cmk, smk, wa, wb, wrecv, a1s, a1r, a2s, a2r, scal,
+    rhs, leg_hbm, waves, wave_rows, obs, ca, sa, cb, sb,
+    x_ref, p_ref, r_ref, s_ref, alpha_ref,
+    leg, z_ref, stage, fsend, frecv, gsend, grecv,
+    tc, ts, ckm, skm, cmk, smk, wa, wb, wsend, wrecv, a1s, a1r, a2s, a2r, scal,
     leg_sem, f_ssem, f_rsem, g_ssem, g_rsem, w_ssem, w_rsem, a1_ssem, a1_rsem, a2_ssem, a2_rsem,
 ):
     me = lax.axis_index("band")
@@ -59,7 +61,10 @@
     core = lax.rem(me, 2)
     worker = me < WORKERS
 
-    wrecv[pl.ds((WSRC - 1) * WROW, WROW), :] = jnp.zeros((WROW, 2 * WCOL), jnp.bfloat16)
+    wrecv[pl.ds((WSRC - 1) * WROW, WROW), :] = jnp.zeros((WROW, NLON), jnp.bfloat16)
+    wsend[...] = jnp.concatenate(
+        [obs[...], jnp.zeros((WROW - SLOTS, NLON), jnp.float32)], axis=0
+    ).astype(jnp.bfloat16)
 
     barrier = pltpu.get_barrier_semaphore()
 
@@ -85,10 +90,12 @@
 
     lax.fori_loop(0, SLOTS, start_leg, 0)
 
+    degree = lax.broadcasted_iota(jnp.int32, (1, LANES), 1)
+
     def mask_slot(s, c):
         for j in range(LATBLOCKS):
             rows = pl.ds(s * 120 + j, 24, stride=5)
-            r_ref[rows, :] = rhs[rows, :] * tri[s, :, 128 * j : 128 * j + 128]
+            r_ref[rows, :] = jnp.where(degree + 128 * j >= waves[me * SLOTS + s], rhs[rows, :], 0.0)
         return c
 
     lax.fori_loop(0, SLOTS, mask_slot, 0)
@@ -119,12 +126,12 @@
             @pl.when(g != me)
             def _():
                 pltpu.make_async_remote_copy(
-                    wts, w_dst(j), w_ssem, w_rsem, device_id={"band": g}, device_id_type=MESH
+                    wsend, w_dst(j), w_ssem, w_rsem, device_id={"band": g}, device_id_type=MESH
                 ).start()
 
             @pl.when(g == me)
             def _():
-                pltpu.make_async_copy(wts, w_dst(j), w_rsem).start()
+                pltpu.make_async_copy(wsend, w_dst(j), w_rsem).start()
 
             return c
 
@@ -169,9 +176,9 @@
             pltpu.make_async_copy(f_block(me), f_dst, f_rsem.at[it]).start()
 
         def f_go(i, c):
-            g = lax.rem(me + spread_offset(i), BANDS)
-
-            @pl.when(g < WORKERS)
+            g = peer(i, zz, yy, core)
+
+            @pl.when(jnp.logical_and(g < WORKERS, g != me))
             def _():
                 pltpu.make_async_remote_copy(
                     f_block(g), f_dst, f_ssem, f_rsem.at[it], device_id={"band": g}, device_id_type=MESH
@@ -179,7 +186,7 @@
 
             return c
 
-        lax.fori_loop(1, BANDS, f_go, 0)
+        lax.fori_loop(0, BANDS, f_go, 0)
 
         @pl.when(it == 0)
         def _():
@@ -188,8 +195,9 @@
                 cosa, sina = ca[a : a + 1, :], sa[a : a + 1, :]
                 tc[32 * a : 32 * a + 32, :] = ((cosa * cb[...] - sina * sb[...]) * norm).astype(jnp.bfloat16)
                 ts[32 * a : 32 * a + 32, :] = ((sina * cb[...] + cosa * sb[...]) * -norm).astype(jnp.bfloat16)
+            wave_row = jnp.concatenate([wave_rows[j : j + 1, :] for j in range(LATBLOCKS)], axis=1)
             pick = (
-                lax.broadcasted_iota(jnp.int32, (MW, MW), 0) == wave_row[...]
+                lax.broadcasted_iota(jnp.int32, (MW, MW), 0) == wave_row
             ).astype(jnp.float32).astype(jnp.bfloat16)
             contract = (((0,), (0,)), ((), ()))
             for src, km, mk in ((tc, ckm, cmk), (ts, skm, smk)):
@@ -221,8 +229,14 @@
             turned = lax.dot_general(
                 wrecv[...], spot, (((0,), (0,)), ((), ())), preferred_element_type=jnp.float32
             )
-            wa[...] = turned[0:KPAD]
-            wb[...] = turned[WCOL : WCOL + KPAD]
+            k_row = lax.broadcasted_iota(jnp.int32, (KPAD, LANES), 0)
+            plus = jnp.where(k_row <= HALF, turned[0:KPAD], 0.0)
+            to_k = lax.broadcasted_iota(jnp.int32, (KPAD, HALF), 0)
+            from_k = lax.broadcasted_iota(jnp.int32, (KPAD, HALF), 1)
+            flip = jnp.logical_and(to_k + from_k == HALF, to_k < HALF).astype(jnp.float32).astype(jnp.bfloat16)
+            mirror = jnp.dot(flip, turned[HALF:].astype(jnp.bfloat16), preferred_element_type=jnp.float32)
+            wa[...] = plus + mirror
+            wb[...] = plus - mirror
 
         scal[3:4, :] = jnp.zeros((1, LANES), jnp.float32)
 
@@ -252,13 +266,17 @@
             pltpu.make_async_copy(g_block(me), g_dst, g_rsem.at[it]).start()
 
             def g_go(i, c):
-                d = lax.rem(me + spread_offset(i), BANDS)
-                pltpu.make_async_remote_copy(
-                    g_block(d), g_dst, g_ssem, g_rsem.at[it], device_id={"band": d}, device_id_type=MESH
-                ).start()
+                d = peer(i, zz, yy, core)
+
+                @pl.when(d != me)
+                def _():
+                    pltpu.make_async_remote_copy(
+                        g_block(d), g_dst, g_ssem, g_rsem.at[it], device_id={"band": d}, device_id_type=MESH
+                    ).start()
+
                 return c
 
-            lax.fori_loop(1, BANDS, g_go, 0)
+            lax.fori_loop(0, BANDS, g_go, 0)
 
         pair = jnp.concatenate([scal[0:1, :], scal[3:4, :]], axis=0)
         own1 = zz * 2 + core
@@ -309,11 +327,12 @@
             out = lax.dot_general(
                 vec, leg[s], (((1,), (1,)), ((), ())), preferred_element_type=jnp.float32
             )
-            out = out * tri[s]
+            wave = waves[me * SLOTS + s]
             base = s * 120
             for j in range(LATBLOCKS):
                 rows = pl.ds(base + j, 24, stride=5)
-                z_ref[rows, :] = r_ref[rows, :] + out[:, 128 * j : 128 * j + 128]
+                adjoint = jnp.where(degree + 128 * j >= wave, out[:, 128 * j : 128 * j + 128], 0.0)
+                z_ref[rows, :] = r_ref[rows, :] + adjoint
             return c
 
         lax.fori_loop(0, SLOTS, backward, 0)
@@ -333,10 +352,14 @@
         along = z_ref[...] + beta * s_ref[...]
         p_ref[...] = direction
         s_ref[...] = along
-        x_ref[...] = x_ref[...] + alpha * direction
-        residual = residual - alpha * along
-        r_ref[...] = residual
-        scal[0:1, :] = jnp.sum(residual * residual, axis=0, keepdims=True)
+
+        @pl.when(it < ITERS - 1)
+        def _():
+            x_ref[...] = x_ref[...] + alpha * direction
+            nxt = residual - alpha * along
+            r_ref[...] = nxt
+            scal[0:1, :] = jnp.sum(nxt * nxt, axis=0, keepdims=True)
+
 
         most = frecv.at[0, pl.ds(0, 59 * MSG)]
 
@@ -356,6 +379,7 @@
         return carry
 
     lax.fori_loop(0, ITERS, iteration, 0)
+    alpha_ref[...] = scal[2:3, :]
 
     def w_sent(j):
         mine = jnp.logical_and(j * LEV <= me, me < j * LEV + LEV)
@@ -378,27 +402,18 @@
 
 
 def on_device(right_side, legendre, wave_map, obs_weight):
-    first_slot = lax.axis_index("band") * SLOTS
-    own_waves = lax.dynamic_slice_in_dim(wave_map, first_slot, SLOTS)
-    tri = (jnp.arange(MW, dtype=jnp.int32)[None, :] >= own_waves[:, None]).astype(jnp.float32)
-    plus = obs_weight[:, : HALF + 1]
-    mirror = jnp.pad(obs_weight[:, : HALF : -1], ((0, 0), (1, 1)))
-    pad = ((0, WROW - SLOTS), (0, WCOL - HALF - 1))
-    wts = jnp.concatenate([jnp.pad(plus + mirror, pad), jnp.pad(plus - mirror, pad)], axis=1).astype(jnp.bfloat16)
     tables = [jnp.asarray(t) for t in small_tables()]
     vmem = pl.BlockSpec(memory_space=pltpu.VMEM)
     f32, bf16 = jnp.float32, jnp.bfloat16
     dma = pltpu.SemaphoreType.DMA
     shape = jax.ShapeDtypeStruct((OWN_ROWS, LANES), f32)
-    x, r = pl.pallas_call(
+    x, p, r, s, alpha = pl.pallas_call(
         kernel,
-        out_shape=(shape, shape),
-        in_specs=[vmem, pl.BlockSpec(memory_space=pl.ANY)] + [vmem] * 7,
-        out_specs=(vmem, vmem),
+        out_shape=(shape, shape, shape, shape, jax.ShapeDtypeStruct((1, LANES), f32)),
+        in_specs=[vmem, pl.BlockSpec(memory_space=pl.ANY), pl.BlockSpec(memory_space=pltpu.SMEM)] + [vmem] * 6,
+        out_specs=(vmem,) * 5,
         scratch_shapes=[
             pltpu.VMEM((SLOTS, MW, MW), bf16),
-            pltpu.VMEM((OWN_ROWS, LANES), f32),
-            pltpu.VMEM((OWN_ROWS, LANES), f32),
             pltpu.VMEM((OWN_ROWS, LANES), f32),
             pltpu.VMEM((BANDS * MSG, LANES), f32),
             pltpu.VMEM((OWN_ROWS, LANES), bf16),
@@ -413,7 +428,8 @@
             pltpu.VMEM((MW, KPAD), bf16),
             pltpu.VMEM((KPAD, LANES), f32),
             pltpu.VMEM((KPAD, LANES), f32),
-            pltpu.VMEM((WSRC * WROW, 2 * WCOL), bf16),
+            pltpu.VMEM((WROW, NLON), bf16),
+            pltpu.VMEM((WSRC * WROW, NLON), bf16),
             pltpu.VMEM((ITERS, 2, LANES), f32),
             pltpu.VMEM((ITERS, 16, 2, LANES), f32),
             pltpu.VMEM((ITERS, 2, LANES), f32),
@@ -423,12 +439,12 @@
             dma((ITERS,)), dma((ITERS,)), dma((ITERS,)), dma((ITERS,)),
         ],
         compiler_params=pltpu.CompilerParams(
-            collective_id=0, has_side_effects=True, vmem_limit_bytes=60 * 1024 * 1024
+            collective_id=0, has_side_effects=True, vmem_limit_bytes=58 * 1024 * 1024
         ),
     )(
-        right_side.reshape(OWN_ROWS, LANES), legendre, tri.reshape(SLOTS, 1, MW), wave_map.reshape(1, MW), wts, *tables
+        right_side.reshape(OWN_ROWS, LANES), legendre, wave_map, wave_map.reshape(LATBLOCKS, LANES), obs_weight, *tables
     )
-    return x.reshape(right_side.shape), r.reshape(right_side.shape)
+    return (x + alpha * p).reshape(right_side.shape), (r - alpha * s).reshape(right_side.shape)
 
 
 def solution(mesh):

time: 129 us -> 116 us (0.90)
  local copies, waits for them, and re-layouts: 7.96 us -> 0 us
  Pallas kernels: 118 us -> 113 us
    pallas_call x1, Pallas kernels: 118 us -> 113 us  [on_device(): pl.pallas_call(kernel, out_shape=(shape, shape, shape, shape, jax.ShapeDt...]
    unnamed x4 -> x0, local copies, waits for them, and re-layouts: 5.07 us -> none
    sub x0 -> x1, other arithmetic: none -> 2.78 us  [on_device(): r - alpha * s]
where the time goes in v2:
time: 116 us
  Pallas kernels  113 us (97%)
  other arithmetic  2.78 us (2%)
    pallas_call x1, Pallas kernels, on_device(): pl.pallas_call(kernel, out_shape=(shape, shape, shape, shape, jax.ShapeDt...  113 us
    sub x1, other arithmetic, on_device(): r - alpha * s  2.78 us

profile of v2, /device:TPU:1, one launch (start us, length us, event | category | flops | bytes accessed | tf_op | source)
XLA Modules:
  0.0 116.1 jit_solution(5180695684016869722)
XLA Ops:
  0.6 112.6 %shard_map.95 = (f32[1200,128]{1,0:T(8,128)}, f32[1200,128]{1,0:T(8,128)}, f32[1200,128]{1,0:T(8,128)}, f32[1200,128]{1,0:T(8,128)}, f32[1,128]{1,0:T(1,128)}) custom-call(f32[1200,128]{1,0:T(8,128)} %bitcast.7, bf16[10,640,640]{2,1,0:T(8,128)(2,1)} %leg_hbm.1, s32[640]{0:T(1024)} %waves.1, s32[5,128]{1,0:T(8,128)} %bitcast.8, f32[10,1280]{1,0:T(8,128)} %obs.1, ...), custom_call_target="tpu_custom_call" | custom-call | tf_op jit(solution)/shard_map/pallas_call | solution.py:410
  113.3 2.8 %multiply_subtract_fusion = (f32[1200,128]{1,0:T(8,128)}, f32[1200,128]{1,0:T(8,128)}) fusion(f32[1200,128]{1,0:T(8,128)} %get-tuple-element.10, f32[1200,128]{1,0:T(8,128)} %get-tuple-element.11, f32[128]{0:T(128)} %bitcast.9, f32[1200,128]{1,0:T(8,128)} %get-tuple-element.7, f32[1200,128]{1,0:T(8,128)} %get-tuple-element.9), kind=kLoop, calls=%fused_computation | loop fusion | flops 614400 | bytes 3686912 | tf_op jit(solution)/shard_map/sub | solution.py:447
